TPU v7x, 32 devices: a whole 2x2x4 slice. The times are simulated.
32 devices in a mesh: shard: 8 (over y, x, core), tensor: 4 (over z).
Axes of the slice: x: 2, y: 2, z: 4, core: 2. Of those that a mesh axis runs over, the one named last changes fastest.
Arguments:
- step: int32 [1], replicated, may hold values from 1 to 19
- lengths: int32 [80], replicated, may hold values from 1 to 262144, 2097152 in all
- grads: bfloat16 [8, 8, 4, 65536], P('shard', None, 'tensor'), may hold values from -2 to 2
- weights: float32 [2097152], P(('shard', 'tensor'))
- moment1: float32 [2097152], P(('shard', 'tensor')), may hold values from -0.4375 to 0.4375
- moment2: float32 [2097152], P(('shard', 'tensor')), may hold values from 0.0001 to 0.01
Outputs:
- new_weights: float32 [2097152], P(('shard', 'tensor'))
- new_moment1: float32 [2097152], P(('shard', 'tensor'))
- new_moment2: float32 [2097152], P(('shard', 'tensor'))
- train_weights: bfloat16 [8, 4, 65536], P(None, 'tensor')
Inputs may be any that keep to these rules, and one draw needn't show every extreme that they name: The lengths sum to 2097152, and one of them equals 262144.
All inputs are finite; a program needn't handle non-finite values.
Results may differ from a plain program's by a relative error of at most 0.0004.
Values may be sent and summed in bfloat16 or wider, within the bound.
No kernel may reach another device: no remote copies, remote signals or barrier semaphores. Data moves between devices by JAX's collectives and lax.ppermute only.
A program may use at most 128 MiB of HBM per device.

v0:
```python
import math
import jax
import jax.numpy as jnp
from jax import lax
from jax.sharding import PartitionSpec as P


def segment_squares(columns, base, starts, ends):
    width = columns.shape[1]
    block = math.gcd(width, 8192)
    blocks = width // block
    pieces = columns.reshape(columns.shape[0], blocks, block).transpose(1, 0, 2)
    places = base + jnp.arange(width, dtype=jnp.int32).reshape(blocks, block)

    def add_block(total, item):
        piece, place = item
        member = ((place[None, :] >= starts[:, None]) & (place[None, :] < ends[:, None])).astype(
            jnp.float32
        )
        return (total + jnp.dot(member, piece.T, precision=lax.Precision.HIGHEST), None)

    init = jnp.zeros((starts.shape[0], columns.shape[0]), jnp.float32)
    total, unused = lax.scan(add_block, init, (pieces, places))
    return total


def spread_ratio(ratio, base, starts, ends, width):
    block = math.gcd(width, 8192)
    blocks = width // block
    places = base + jnp.arange(width, dtype=jnp.int32).reshape(blocks, block)

    def expand(carry, place):
        member = ((place[None, :] >= starts[:, None]) & (place[None, :] < ends[:, None])).astype(
            jnp.float32
        )
        return (carry, jnp.dot(ratio[None, :], member, precision=lax.Precision.HIGHEST)[0])

    unused, rows = lax.scan(expand, jnp.float32(0.0), places)
    return rows.reshape(width)


def local(step, lengths, grads, weights, moment1, moment2):
    width = weights.shape[0]
    base = (lax.axis_index("shard") * lax.axis_size("tensor") + lax.axis_index("tensor")) * width
    ends = jnp.cumsum(lengths)
    starts = ends - lengths
    flat_grads = grads.reshape(-1)
    grad = lax.psum_scatter(
        flat_grads.astype(jnp.float32), "shard", scatter_dimension=0, tiled=True
    )
    count = step[0].astype(jnp.float32)
    first = 1.0 - jnp.power(jnp.float32(0.9), count)
    second = 1.0 - jnp.power(jnp.float32(0.999), count)
    new_moment1 = 0.9 * moment1 + 0.1 * grad
    new_moment2 = 0.999 * moment2 + 0.001 * grad * grad
    update = new_moment1 / first / (jnp.sqrt(new_moment2 / second) + 1e-06) + 0.1 * weights
    stacked = jnp.stack([weights * weights, update * update])
    partial_value = segment_squares(stacked, base, starts, ends)
    wsq, usq = lax.psum((partial_value[:, 0], partial_value[:, 1]), ("shard", "tensor"))
    ratio = jnp.sqrt(wsq) / jnp.maximum(jnp.sqrt(usq), 1.0)
    local_ratio = spread_ratio(ratio, base, starts, ends, width)
    new_weights = weights - 0.25 * local_ratio * update
    rounded = new_weights.astype(jnp.bfloat16).reshape(1, 1, width)
    train_weights = lax.all_gather(rounded, "shard", axis=0, tiled=True)
    return (new_weights, new_moment1, new_moment2, train_weights)


def solution(mesh):
    placed = (
        P(),
        P(),
        P("shard", None, "tensor", None),
        P(("shard", "tensor")),
        P(("shard", "tensor")),
        P(("shard", "tensor")),
    )
    return jax.shard_map(
        local,
        mesh=mesh,
        in_specs=placed,
        out_specs=(
            P(("shard", "tensor")),
            P(("shard", "tensor")),
            P(("shard", "tensor")),
            P(None, "tensor", None),
        ),
        check_vma=False,
    )
```

profile of v0, /device:TPU:0, one launch (start us, length us, event | category | flops | bytes accessed | tf_op | source)
XLA Modules:
  0.0 172.9 jit_solution(6423546391148193087)
XLA Ops:
  7.2 0.0 all-reduce.4.cloned.1.call-start
  7.2 1.4 convert_bitcast_fusion
  8.6 1.7 copy.13
  10.3 0.0 copy-start.5
  10.3 0.0 copy-start.6
  10.3 0.0 copy-start
  10.3 0.0 copy-start.3
  10.3 0.0 copy-start.4
  10.3 0.0 all-reduce.4.cloned.1.call-update
  10.3 0.0 all-gather.3.cloned.1.call-start
  11.2 0.0 copy-done.5
  11.2 0.1 copy.12
  11.3 0.1 reduce-window.9
  11.4 0.1 reduce
  11.6 0.0 copy-done.6
  11.6 0.6 dynamic-slice
  12.9 62.5 %all-reduce.4.cloned.1.call-done = f32[524288]{0:T(1024)} async-done(((f32[524288]{0:T(1024)}), f32[524288]{0:T(1024)}) %all-reduce.4.cloned.1.call-update) | async-done | bytes 2097168
  75.4 0.0 copy-done
  75.4 0.0 copy-done.3
  75.4 0.0 copy-done.4
  75.4 1.2 fusion.14
  76.5 0.0 copy-start.1
  76.6 0.0 copy-start.2
  76.6 0.5 maximum_bitcast_fusion
  77.0 12.3 %while.22 = (s32[]{:T(128)}, f32[80,2]{0,1:T(2,128)S(1)}, s32[8,8192]{1,0:T(8,128)S(1)}, s32[80]{0:T(128)S(1)}, s32[80]{0:T(128)S(1)}, /*index=5*/f32[8,2,8192]{2,1,0:T(2,128)S(1)}, s32[]{:T(128)}, s32[]{:T(128)}) while((s32[]{:T(128)}, f32[80,2]{0,1:T(2,128)S(1)}, s32[8,8192]{1,0:T(8,128)S(1)}, s32[80]{0:T(128)S(1)}, ...), condition=%wide.region_3.4_spmd.clone, body=%wide.region_2.3_spmd.clone.sunk | while | flops 17695044 | bytes 166631 | solution.py:23
  77.1 1.5 fusion.24
  78.6 1.5 fusion.24
  80.2 1.5 fusion.24
  81.7 1.5 fusion.24
  83.2 1.5 fusion.24
  84.8 1.5 fusion.24
  86.3 1.5 fusion.24
  87.9 1.5 fusion.24
  89.4 39.4 %all-reduce.1 = (f32[80]{0:T(128)S(1)}, f32[80]{0:T(128)S(1)}) all-reduce(f32[80]{0:T(128)S(1)} %get-tuple-element.124, f32[80]{0:T(128)S(1)} %get-tuple-element.123), channel_id=1, replica_groups=mesh['shard'=8,'tensor'=4] {'shard','tensor'}, use_global_device_ids=true, to_apply=%region_5.6 | all-reduce | flops 160 | bytes 1280 | tf_op jit(solution)/shard_map/psum | solution.py:59
  128.7 10.2 %while.21 = (s32[]{:T(128)}, f32[8,8192]{1,0:T(8,128)S(1)}, s32[8,8192]{1,0:T(8,128)S(1)}, s32[80]{0:T(128)S(1)}, s32[80]{0:T(128)S(1)}, /*index=5*/f32[80]{0:T(128)S(1)}, s32[]{:T(128)}, s32[]{:T(128)}) while((s32[]{:T(128)}, f32[8,8192]{1,0:T(8,128)S(1)}, s32[8,8192]{1,0:T(8,128)S(1)}, s32[80]{0:T(128)S(1)}, s32[80]{0:T(128)S(1)}, ...), condition=%wide.region_7.8_spmd, body=%wide.region_6.7_spmd.sunk | while | flops 9830402 | bytes 197661 | solution.py:38
  128.8 1.1 fusion.22
  129.9 0.1 dynamic_update_slice.5
  130.1 1.1 fusion.22
  131.1 0.1 dynamic_update_slice.5
  131.3 1.1 fusion.22
  132.4 0.1 dynamic_update_slice.5
  132.6 1.1 fusion.22
  133.7 0.1 dynamic_update_slice.5
  133.9 1.1 fusion.22
  134.9 0.1 dynamic_update_slice.5
  135.1 1.1 fusion.22
  136.2 0.1 dynamic_update_slice.5
  136.4 1.1 fusion.22
  137.5 0.1 dynamic_update_slice.5
  137.7 1.1 fusion.22
  138.7 0.1 dynamic_update_slice.5
  138.9 0.1 copy.14
  139.0 0.0 copy-done.1
  139.0 0.0 copy-done.2
  139.0 0.9 fusion.15
  139.9 0.0 all-gather.3.cloned.1.call-update
  140.0 23.5 %all-gather.3.cloned.1.call-done = bf16[524288]{0:T(1024)(128)(2,1)} async-done(((bf16[65536]{0:T(1024)(128)(2,1)}), bf16[524288]{0:T(1024)(128)(2,1)}) %all-gather.3.cloned.1.call-update) | async-done | bytes 1048592 | tf_op jit(solution)/shard_map/all_gather | solution.py:64
  163.5 2.6 %reshape.79 = bf16[8,1,65536]{2,0,1:T(8,128)(2,1)} reshape(bf16[524288]{0:T(1024)(128)(2,1)} %all-gather.3.cloned.1.call-done) | data formatting | bytes 2097152 | tf_op jit(solution)/shard_map/all_gather | solution.py:64
  (23 shorter events, 0.5 us)
Async XLA Ops:
  7.2 68.2 %all-reduce.4.cloned.1.call-start = ((), (), s32[]{:S(2)}) async-start(), calls=%async_computation.1 | async-start | bytes 4194304
  10.3 0.9 copy-start.5
  10.3 1.3 copy-start.6
  10.3 65.1 %copy-start = (f32[65536]{0:T(1024)S(1)}, f32[65536]{0:T(1024)}, u32[]{:S(2)}) copy-start(f32[65536]{0:T(1024)} %param.13) | copy-start | bytes 786436
  10.3 65.1 %copy-start.3 = (f32[65536]{0:T(1024)S(1)}, f32[65536]{0:T(1024)}, u32[]{:S(2)}) copy-start(f32[65536]{0:T(1024)} %param.15) | copy-start | bytes 786436
  10.3 65.1 %copy-start.4 = (f32[65536]{0:T(1024)S(1)}, f32[65536]{0:T(1024)}, u32[]{:S(2)}) copy-start(f32[65536]{0:T(1024)} %param.14) | copy-start | bytes 786436
  10.3 153.2 %all-gather.3.cloned.1.call-start = ((), (), s32[]{:S(2)}) async-start(), calls=%async_computation | async-start | bytes 1179648 | tf_op jit(solution)/shard_map/all_gather | solution.py:64
  76.5 62.5 %copy-start.1 = (f32[65536]{0:T(1024)}, f32[65536]{0:T(1024)S(1)}, u32[]{:S(2)}) copy-start(f32[65536]{0:T(1024)S(1)} %get-tuple-element.120) | copy-start | bytes 786436
  76.6 62.5 %copy-start.2 = (f32[65536]{0:T(1024)}, f32[65536]{0:T(1024)S(1)}, u32[]{:S(2)}) copy-start(f32[65536]{0:T(1024)S(1)} %get-tuple-element.121) | copy-start | bytes 786436
Sparse Core Ops, SparseCore 0:
  11.2 64.0 all-reduce.3
  140.1 23.3 all-gather.2
where the time goes:
time: 173 us
  waiting for transfers between devices  86.1 us (50%)
  blocking collectives  39.4 us (23%)
  matrix products  20.4 us (12%)
  between operations  15.7 us (9%)
  local copies, waits for them, and re-layouts  6.7 us (4%)
  other arithmetic  4.19 us (2%)
    unnamed x3, waiting for transfers between devices  62.5 us
    psum x1, blocking collectives, local(): lax.psum((partial_value[:, 0], partial_value[:, 1]), ('shard', 'tensor'))  39.4 us
    all_gather x1, waiting for transfers between devices, local(): train_weights = lax.all_gather(rounded, 'shard', axis=0, tiled=True)  23.5 us
    dot_general x8, matrix products, add_block(): jnp.dot(member, piece.T, precision=lax.Precision.HIGHEST)  11.8 us
    dot_general x8, matrix products, expand(): jnp.dot(ratio[None, :], member, precision=lax.Precision.HIGHEST)[0]  8.56 us
  transfers between devices with their start and end apart: 2, of which 2 were waited for; matrix products, arithmetic and copies ran while one was open for 1% of the time, Pallas kernels for 0%

commit v1 on v0

--- a/solution.py
+++ b/solution.py
@@ -61,7 +61,34 @@
     local_ratio = spread_ratio(ratio, base, starts, ends, width)
     new_weights = weights - 0.25 * local_ratio * update
     rounded = new_weights.astype(jnp.bfloat16).reshape(1, 1, width)
-    train_weights = lax.all_gather(rounded, "shard", axis=0, tiled=True)
+    f_next, res, left_arr = (
+        jax.lax.psum(1, "shard"),
+        jax.lax.axis_index("shard"),
+        rounded.shape[0],
+    )
+    chunks = []
+    for num, s in enumerate(rounded.shape):
+        chunks.append(s * f_next if num == 0 else s)
+    train_weights = lax.dynamic_update_slice_in_dim(
+        jnp.zeros(chunks, rounded.dtype), rounded, res * left_arr, axis=0
+    )
+    newest = reached = rounded
+    for h in range(1, f_next // 2 + 1):
+        pages = []
+        for num in range(f_next):
+            pages.append((num, (num + 1) % f_next))
+        newest = jax.lax.ppermute(newest, "shard", pages)
+        train_weights = lax.dynamic_update_slice_in_dim(
+            train_weights, newest, (res - h) % f_next * left_arr, axis=0
+        )
+        if 2 * h < f_next:
+            made = []
+            for num in range(f_next):
+                made.append((num, (num - 1) % f_next))
+            reached = jax.lax.ppermute(reached, "shard", made)
+            train_weights = lax.dynamic_update_slice_in_dim(
+                train_weights, reached, (res + h) % f_next * left_arr, axis=0
+            )
     return (new_weights, new_moment1, new_moment2, train_weights)
 
 

time: 173 us -> 211 us (1.22); the launches traced: 173 us -> 209 us
  local copies, waits for them, and re-layouts: 6.7 us -> 40.6 us
  starting transfers between devices: 0.08 us -> 8.23 us
  waiting for transfers between devices: 86.1 us -> 79.7 us
    dynamic_update_slice x0 -> x8, local copies, waits for them, and re-layouts: none -> 35.4 us  [the longest x4 17.7 us: local(): lax.dynamic_update_slice_in_dim(train_weights, newest, (res - h) % f_next...]
    all_gather x1 -> x0, waiting for transfers between devices: 23.5 us -> none  [local(): train_weights = lax.all_gather(rounded, 'shard', axis=0, tiled=True)]
    ppermute x0 -> x7, waiting for transfers between devices: none -> 17.1 us  [the longest x4 16.5 us: local(): newest = jax.lax.ppermute(newest, 'shard', pages)]
    ppermute x0 -> x7, starting transfers between devices: none -> 8.19 us  [the longest x3 8.12 us: local(): reached = jax.lax.ppermute(reached, 'shard', made)]
    all_gather x1 -> x0, local copies, waits for them, and re-layouts: 2.64 us -> none  [local(): train_weights = lax.all_gather(rounded, 'shard', axis=0, tiled=True)]
    unnamed x3 -> x2, waiting for transfers between devices: 62.5 us -> 62.6 us
  transfers between devices with their start and end apart: 2 -> 8, of which waited for: 2 -> 5; matrix products, arithmetic and copies ran while one was open for 1% -> 15% of each run, Pallas kernels for 0% -> 0%
where the time goes in v1:
time: 211 us; the launch traced here: 209 us
  waiting for transfers between devices  79.7 us (38%)
  local copies, waits for them, and re-layouts  40.6 us (19%)
  blocking collectives  39.3 us (19%)
  matrix products  20.4 us (10%)
  between operations  15.8 us (7%)
  starting transfers between devices  8.23 us (4%)
  other arithmetic  4.14 us (2%)
    unnamed x2, waiting for transfers between devices  62.6 us
    psum x1, blocking collectives, local(): lax.psum((partial_value[:, 0], partial_value[:, 1]), ('shard', 'tensor'))  39.3 us
    dynamic_update_slice x4, local copies, waits for them, and re-layouts, local(): lax.dynamic_update_slice_in_dim(train_weights, newest, (res - h) % f_next...  17.7 us
    ppermute x4, waiting for transfers between devices, local(): newest = jax.lax.ppermute(newest, 'shard', pages)  16.5 us
    dynamic_update_slice x3, local copies, waits for them, and re-layouts, local(): lax.dynamic_update_slice_in_dim(train_weights, reached, (res + h) % f_nex...  13.3 us
    dot_general x8, matrix products, add_block(): jnp.dot(member, piece.T, precision=lax.Precision.HIGHEST)  11.8 us
    dot_general x8, matrix products, expand(): jnp.dot(ratio[None, :], member, precision=lax.Precision.HIGHEST)[0]  8.56 us
    ppermute x3, starting transfers between devices, local(): reached = jax.lax.ppermute(reached, 'shard', made)  8.12 us
  transfers between devices with their start and end apart: 8, of which 5 were waited for; matrix products, arithmetic and copies ran while one was open for 15% of the time, Pallas kernels for 0%

profile of v1, /device:TPU:0, one launch (start us, length us, event | category | flops | bytes accessed | tf_op | source)
XLA Modules:
  0.0 208.7 jit_solution(12174275310416380953)
XLA Ops:
  7.2 0.0 all-reduce.4.cloned.1.call-start
  7.2 1.4 convert_bitcast_fusion
  8.6 1.7 copy.13
  10.3 0.0 copy-start.5
  10.3 0.0 all-reduce.4.cloned.1.call-update
  11.2 0.1 copy.12
  11.3 0.1 reduce-window.9
  11.4 0.1 reduce
  11.5 0.6 dynamic-slice
  12.8 62.6 %all-reduce.4.cloned.1.call-done = f32[524288]{0:T(1024)} async-done(((f32[524288]{0:T(1024)}), f32[524288]{0:T(1024)}) %all-reduce.4.cloned.1.call-update) | async-done | bytes 2097168
  75.4 1.2 fusion.14
  76.6 0.0 copy-start.1
  76.6 0.0 copy-start.2
  76.6 0.5 maximum_bitcast_fusion
  77.1 12.3 %while.22 = (s32[]{:T(128)}, f32[80,2]{0,1:T(2,128)S(1)}, s32[8,8192]{1,0:T(8,128)S(1)}, s32[80]{0:T(128)S(1)}, s32[80]{0:T(128)S(1)}, /*index=5*/f32[8,2,8192]{2,1,0:T(2,128)S(1)}, s32[]{:T(128)}, s32[]{:T(128)}) while((s32[]{:T(128)}, f32[80,2]{0,1:T(2,128)S(1)}, s32[8,8192]{1,0:T(8,128)S(1)}, s32[80]{0:T(128)S(1)}, ...), condition=%wide.region_3.4_spmd.clone, body=%wide.region_2.3_spmd.clone.sunk | while | flops 17695044 | bytes 166631 | solution.py:23
  77.1 1.5 fusion.24
  78.7 1.5 fusion.24
  80.2 1.5 fusion.24
  81.8 1.5 fusion.24
  83.3 1.5 fusion.24
  84.8 1.5 fusion.24
  86.4 1.5 fusion.24
  87.9 1.5 fusion.24
  89.4 39.3 %all-reduce.1 = (f32[80]{0:T(128)S(1)}, f32[80]{0:T(128)S(1)}) all-reduce(f32[80]{0:T(128)S(1)} %get-tuple-element.124, f32[80]{0:T(128)S(1)} %get-tuple-element.123), channel_id=1, replica_groups=mesh['shard'=8,'tensor'=4] {'shard','tensor'}, use_global_device_ids=true, to_apply=%region_5.6 | all-reduce | flops 160 | bytes 1280 | tf_op jit(solution)/shard_map/psum | solution.py:59
  128.8 10.2 %while.21 = (s32[]{:T(128)}, f32[8,8192]{1,0:T(8,128)S(1)}, s32[8,8192]{1,0:T(8,128)S(1)}, s32[80]{0:T(128)S(1)}, s32[80]{0:T(128)S(1)}, /*index=5*/f32[80]{0:T(128)S(1)}, s32[]{:T(128)}, s32[]{:T(128)}) while((s32[]{:T(128)}, f32[8,8192]{1,0:T(8,128)S(1)}, s32[8,8192]{1,0:T(8,128)S(1)}, s32[80]{0:T(128)S(1)}, s32[80]{0:T(128)S(1)}, ...), condition=%wide.region_7.8_spmd, body=%wide.region_6.7_spmd.sunk | while | flops 9830402 | bytes 197661 | solution.py:38
  128.8 1.1 fusion.22
  129.9 0.1 dynamic_update_slice.37
  130.1 1.1 fusion.22
  131.2 0.1 dynamic_update_slice.37
  131.4 1.1 fusion.22
  132.4 0.1 dynamic_update_slice.37
  132.6 1.1 fusion.22
  133.7 0.1 dynamic_update_slice.37
  133.9 1.1 fusion.22
  135.0 0.1 dynamic_update_slice.37
  135.2 1.1 fusion.22
  136.3 0.1 dynamic_update_slice.37
  136.5 1.1 fusion.22
  137.5 0.1 dynamic_update_slice.37
  137.7 1.1 fusion.22
  138.8 0.1 dynamic_update_slice.37
  139.0 0.1 copy.14
  139.1 0.9 fusion.15
  139.9 0.1 reshape.77
  140.1 0.1 collective-permute-start
  140.1 2.6 %collective-permute-start.1 = (bf16[1,1,65536]{2,0,1:T(2,128)(2,1)S(1)}, bf16[1,1,65536]{2,0,1:T(2,128)(2,1)S(1)}, u32[]{:S(2)}, u32[]{:S(2)}) collective-permute-start(bf16[1,1,65536]{2,0,1:T(2,128)(2,1)S(1)} %reshape.77), channel_id=1, source_target_pairs={{0,28},{4,0},{8,4},{12,8},{16,12},{20,16},{24,20},{28,24},{1,29},{... | collective-permute-start | bytes 393224 | tf_op jit(solution)/shard_map/ppermute | solution.py:88
  142.8 5.1 %collective-permute-done = bf16[1,1,65536]{2,0,1:T(2,128)(2,1)S(1)} collective-permute-done((bf16[1,1,65536]{2,0,1:T(2,128)(2,1)S(1)}, bf16[1,1,65536]{2,0,1:T(2,128)(2,1)S(1)}, u32[]{:S(2)}, u32[]{:S(2)}) %collective-permute-start) | collective-permute-done | bytes 131104 | tf_op jit(solution)/shard_map/ppermute | solution.py:80
  147.9 0.6 collective-permute-done.1
  148.5 2.8 %collective-permute-start.3 = (bf16[1,1,65536]{2,0,1:T(2,128)(2,1)S(1)}, bf16[1,1,65536]{2,0,1:T(2,128)(2,1)S(1)}, u32[]{:S(2)}, u32[]{:S(2)}) collective-permute-start(bf16[1,1,65536]{2,0,1:T(2,128)(2,1)S(1)} %collective-permute-done.1), channel_id=1, source_target_pairs={{0,28},{4,0},{8,4},{12,8},{16,12},{20,16},{24,20},{28,24},{1,29},{... | collective-permute-start | bytes 393224 | tf_op jit(solution)/shard_map/ppermute | solution.py:88
  151.3 5.0 %collective-permute-done.2 = bf16[1,1,65536]{2,0,1:T(2,128)(2,1)S(1)} collective-permute-done((bf16[1,1,65536]{2,0,1:T(2,128)(2,1)S(1)}, bf16[1,1,65536]{2,0,1:T(2,128)(2,1)S(1)}, u32[]{:S(2)}, u32[]{:S(2)}) %collective-permute-start.2) | collective-permute-done | bytes 131104 | tf_op jit(solution)/shard_map/ppermute | solution.py:80
  156.3 0.0 collective-permute-start.4
  156.3 2.7 %collective-permute-start.5 = (bf16[1,1,65536]{2,0,1:T(2,128)(2,1)S(1)}, bf16[1,1,65536]{2,0,1:T(2,128)(2,1)S(1)}, u32[]{:S(2)}, u32[]{:S(2)}) collective-permute-start(bf16[1,1,65536]{2,0,1:T(2,128)(2,1)S(1)} %collective-permute-done.3), channel_id=1, source_target_pairs={{0,28},{4,0},{8,4},{12,8},{16,12},{20,16},{24,20},{28,24},{1,29},{... | collective-permute-start | bytes 393224 | tf_op jit(solution)/shard_map/ppermute | solution.py:88
  159.0 6.4 %collective-permute-done.4 = bf16[1,1,65536]{2,0,1:T(2,128)(2,1)S(1)} collective-permute-done((bf16[1,1,65536]{2,0,1:T(2,128)(2,1)S(1)}, bf16[1,1,65536]{2,0,1:T(2,128)(2,1)S(1)}, u32[]{:S(2)}, u32[]{:S(2)}) %collective-permute-start.4) | collective-permute-done | bytes 131104 | tf_op jit(solution)/shard_map/ppermute | solution.py:80
  165.3 0.1 broadcast_in_dim.13
  165.4 4.4 %dynamic_update_slice.28 = bf16[8,1,65536]{2,0,1:T(8,128)(2,1)S(1)} dynamic-update-slice(bf16[8,1,65536]{2,0,1:T(8,128)(2,1)S(1)} %broadcast_in_dim.13, bf16[1,1,65536]{2,0,1:T(2,128)(2,1)S(1)} %reshape.77, s32[]{:T(128)S(6)} %select_n.55, s32[]{:T(128)} %constant.88.clone.1, s32[]{:T(128)} %constant.88.clone.1) | dynamic-update-slice | bytes 262148 | tf_op jit(solution)/shard_map/dynamic_update_slice | solution.py:72
  169.9 4.4 %dynamic_update_slice.29 = bf16[8,1,65536]{2,0,1:T(8,128)(2,1)S(1)} dynamic-update-slice(bf16[8,1,65536]{2,0,1:T(8,128)(2,1)S(1)} %dynamic_update_slice.28, bf16[1,1,65536]{2,0,1:T(2,128)(2,1)S(1)} %collective-permute-done, s32[]{:T(128)S(6)} %select_n.57, s32[]{:T(128)} %constant.88.clone.1, s32[]{:T(128)} %constant.88.clone.1) | dynamic-update-slice | bytes 262148 | tf_op jit(solution)/shard_map/dynamic_update_slice | solution.py:81
  174.3 4.4 %dynamic_update_slice.30 = bf16[8,1,65536]{2,0,1:T(8,128)(2,1)S(1)} dynamic-update-slice(bf16[8,1,65536]{2,0,1:T(8,128)(2,1)S(1)} %dynamic_update_slice.29, bf16[1,1,65536]{2,0,1:T(2,128)(2,1)S(1)} %collective-permute-done.1, s32[]{:T(128)S(6)} %select_n.59, s32[]{:T(128)} %constant.88.clone.1, s32[]{:T(128)} %constant.88.clone.1) | dynamic-update-slice | bytes 262148 | tf_op jit(solution)/shard_map/dynamic_update_slice | solution.py:89
  178.7 4.4 %dynamic_update_slice.31 = bf16[8,1,65536]{2,0,1:T(8,128)(2,1)S(1)} dynamic-update-slice(bf16[8,1,65536]{2,0,1:T(8,128)(2,1)S(1)} %dynamic_update_slice.30, bf16[1,1,65536]{2,0,1:T(2,128)(2,1)S(1)} %collective-permute-done.2, s32[]{:T(128)S(6)} %select_n.61, s32[]{:T(128)} %constant.88.clone.1, s32[]{:T(128)} %constant.88.clone.1) | dynamic-update-slice | bytes 262148 | tf_op jit(solution)/shard_map/dynamic_update_slice | solution.py:81
  183.1 4.4 %dynamic_update_slice.32 = bf16[8,1,65536]{2,0,1:T(8,128)(2,1)S(1)} dynamic-update-slice(bf16[8,1,65536]{2,0,1:T(8,128)(2,1)S(1)} %dynamic_update_slice.31, bf16[1,1,65536]{2,0,1:T(2,128)(2,1)S(1)} %collective-permute-done.3, s32[]{:T(128)S(6)} %select_n.63, s32[]{:T(128)} %constant.88.clone.1, s32[]{:T(128)} %constant.88.clone.1) | dynamic-update-slice | bytes 262148 | tf_op jit(solution)/shard_map/dynamic_update_slice | solution.py:89
  187.6 4.4 %dynamic_update_slice.33 = bf16[8,1,65536]{2,0,1:T(8,128)(2,1)S(1)} dynamic-update-slice(bf16[8,1,65536]{2,0,1:T(8,128)(2,1)S(1)} %dynamic_update_slice.32, bf16[1,1,65536]{2,0,1:T(2,128)(2,1)S(1)} %collective-permute-done.4, s32[]{:T(128)S(6)} %select_n.65, s32[]{:T(128)} %constant.88.clone.1, s32[]{:T(128)} %constant.88.clone.1) | dynamic-update-slice | bytes 262148 | tf_op jit(solution)/shard_map/dynamic_update_slice | solution.py:81
  192.0 4.4 %dynamic_update_slice.34 = bf16[8,1,65536]{2,0,1:T(8,128)(2,1)S(1)} dynamic-update-slice(bf16[8,1,65536]{2,0,1:T(8,128)(2,1)S(1)} %dynamic_update_slice.33, bf16[1,1,65536]{2,0,1:T(2,128)(2,1)S(1)} %collective-permute-done.5, s32[]{:T(128)S(6)} %select_n.67, s32[]{:T(128)} %constant.88.clone.1, s32[]{:T(128)} %constant.88.clone.1) | dynamic-update-slice | bytes 262148 | tf_op jit(solution)/shard_map/dynamic_update_slice | solution.py:89
  196.5 4.4 %dynamic_update_slice.35 = bf16[8,1,65536]{2,0,1:T(8,128)(2,1)S(1)} dynamic-update-slice(bf16[8,1,65536]{2,0,1:T(8,128)(2,1)S(1)} %dynamic_update_slice.34, bf16[1,1,65536]{2,0,1:T(2,128)(2,1)S(1)} %collective-permute-done.6, s32[]{:T(128)S(6)} %select_n.69, s32[]{:T(128)} %constant.88.clone.1, s32[]{:T(128)} %constant.88.clone.1) | dynamic-update-slice | bytes 262148 | tf_op jit(solution)/shard_map/dynamic_update_slice | solution.py:81
  200.9 0.0 copy-start.3
  200.9 1.0 copy-done.3
  (39 shorter events, 0.5 us)
Async XLA Ops:
  7.2 68.3 %all-reduce.4.cloned.1.call-start = ((), (), s32[]{:S(2)}) async-start(), calls=%async_computation | async-start | bytes 4194304
  10.3 0.9 copy-start.6
  10.3 1.2 copy-start.7
  10.3 65.2 %copy-start = (f32[65536]{0:T(1024)S(1)}, f32[65536]{0:T(1024)}, u32[]{:S(2)}) copy-start(f32[65536]{0:T(1024)} %param.13) | copy-start | bytes 786436
  10.3 65.2 %copy-start.4 = (f32[65536]{0:T(1024)S(1)}, f32[65536]{0:T(1024)}, u32[]{:S(2)}) copy-start(f32[65536]{0:T(1024)} %param.15) | copy-start | bytes 786436
  10.3 65.2 %copy-start.5 = (f32[65536]{0:T(1024)S(1)}, f32[65536]{0:T(1024)}, u32[]{:S(2)}) copy-start(f32[65536]{0:T(1024)} %param.14) | copy-start | bytes 786436
  76.6 62.4 %copy-start.1 = (f32[65536]{0:T(1024)}, f32[65536]{0:T(1024)S(1)}, u32[]{:S(2)}) copy-start(f32[65536]{0:T(1024)S(1)} %get-tuple-element.120) | copy-start | bytes 786436
  76.6 62.4 %copy-start.2 = (f32[65536]{0:T(1024)}, f32[65536]{0:T(1024)S(1)}, u32[]{:S(2)}) copy-start(f32[65536]{0:T(1024)S(1)} %get-tuple-element.121) | copy-start | bytes 786436
  140.1 7.8 %collective-permute-start = (bf16[1,1,65536]{2,0,1:T(2,128)(2,1)S(1)}, bf16[1,1,65536]{2,0,1:T(2,128)(2,1)S(1)}, u32[]{:S(2)}, u32[]{:S(2)}) collective-permute-start(bf16[1,1,65536]{2,0,1:T(2,128)(2,1)S(1)} %reshape.77), channel_id=1, source_target_pairs={{0,4},{4,8},{8,12},{12,16},{16,20},{20,24},{24,28},{28,0},{1,5},{5... | collective-permute-start | bytes 393224 | tf_op jit(solution)/shard_map/ppermute | solution.py:80
  140.1 8.4 %collective-permute-start.1 = (bf16[1,1,65536]{2,0,1:T(2,128)(2,1)S(1)}, bf16[1,1,65536]{2,0,1:T(2,128)(2,1)S(1)}, u32[]{:S(2)}, u32[]{:S(2)}) collective-permute-start(bf16[1,1,65536]{2,0,1:T(2,128)(2,1)S(1)} %reshape.77), channel_id=1, source_target_pairs={{0,28},{4,0},{8,4},{12,8},{16,12},{20,16},{24,20},{28,24},{1,29},{... | collective-permute-start | bytes 393224 | tf_op jit(solution)/shard_map/ppermute | solution.py:88
  147.9 8.4 %collective-permute-start.2 = (bf16[1,1,65536]{2,0,1:T(2,128)(2,1)S(1)}, bf16[1,1,65536]{2,0,1:T(2,128)(2,1)S(1)}, u32[]{:S(2)}, u32[]{:S(2)}) collective-permute-start(bf16[1,1,65536]{2,0,1:T(2,128)(2,1)S(1)} %collective-permute-done), channel_id=1, source_target_pairs={{0,4},{4,8},{8,12},{12,16},{16,20},{20,24},{24,28},{28,0},{1,5},{5... | collective-permute-start | bytes 393224 | tf_op jit(solution)/shard_map/ppermute | solution.py:80
  148.5 7.8 %collective-permute-start.3 = (bf16[1,1,65536]{2,0,1:T(2,128)(2,1)S(1)}, bf16[1,1,65536]{2,0,1:T(2,128)(2,1)S(1)}, u32[]{:S(2)}, u32[]{:S(2)}) collective-permute-start(bf16[1,1,65536]{2,0,1:T(2,128)(2,1)S(1)} %collective-permute-done.1), channel_id=1, source_target_pairs={{0,28},{4,0},{8,4},{12,8},{16,12},{20,16},{24,20},{28,24},{1,29},{... | collective-permute-start | bytes 393224 | tf_op jit(solution)/shard_map/ppermute | solution.py:88
  156.3 9.1 %collective-permute-start.4 = (bf16[1,1,65536]{2,0,1:T(2,128)(2,1)S(1)}, bf16[1,1,65536]{2,0,1:T(2,128)(2,1)S(1)}, u32[]{:S(2)}, u32[]{:S(2)}) collective-permute-start(bf16[1,1,65536]{2,0,1:T(2,128)(2,1)S(1)} %collective-permute-done.2), channel_id=1, source_target_pairs={{0,4},{4,8},{8,12},{12,16},{16,20},{20,24},{24,28},{28,0},{1,5},{5... | collective-permute-start | bytes 393224 | tf_op jit(solution)/shard_map/ppermute | solution.py:80
  156.3 35.7 %collective-permute-start.5 = (bf16[1,1,65536]{2,0,1:T(2,128)(2,1)S(1)}, bf16[1,1,65536]{2,0,1:T(2,128)(2,1)S(1)}, u32[]{:S(2)}, u32[]{:S(2)}) collective-permute-start(bf16[1,1,65536]{2,0,1:T(2,128)(2,1)S(1)} %collective-permute-done.3), channel_id=1, source_target_pairs={{0,28},{4,0},{8,4},{12,8},{16,12},{20,16},{24,20},{28,24},{1,29},{... | collective-permute-start | bytes 393224 | tf_op jit(solution)/shard_map/ppermute | solution.py:88
  165.3 31.1 %collective-permute-start.6 = (bf16[1,1,65536]{2,0,1:T(2,128)(2,1)S(1)}, bf16[1,1,65536]{2,0,1:T(2,128)(2,1)S(1)}, u32[]{:S(2)}, u32[]{:S(2)}) collective-permute-start(bf16[1,1,65536]{2,0,1:T(2,128)(2,1)S(1)} %collective-permute-done.4), channel_id=1, source_target_pairs={{0,4},{4,8},{8,12},{12,16},{16,20},{20,24},{24,28},{28,0},{1,5},{5... | collective-permute-start | bytes 393224 | tf_op jit(solution)/shard_map/ppermute | solution.py:80
  200.9 1.0 copy-start.3
Sparse Core Ops, SparseCore 0:
  11.2 64.1 all-reduce.3
